TPU v7x, 128 devices: a whole 4x4x4 slice. The times are simulated.
128 devices in a mesh: rcv: 16 (over x_hi, y, core), src: 8 (over z, x_lo).
Axes of the slice: x: 4 (x_hi: 2, x_lo: 2; x = x_hi * 2 + x_lo), y: 4, z: 4, core: 2. Of those that a mesh axis runs over, the one named last changes fastest.
Arguments:
- kernel_codes: bfloat16 [2, 8192, 65536], P(None, 'rcv', 'src'), may hold values from -128 to 127
- kernel_exps: int32 [8192, 512], P('rcv', 'src'), may hold values from -17 to -14
- wavefield: bfloat16 [2, 65536, 128], P(None, 'src', 'rcv'), may hold values from -6 to 6
- observed: bfloat16 [2, 8192, 128], P(None, 'rcv'), may hold values from -6 to 6
- receiver_mask: int32 [8192], P('rcv'), may hold values 0 or 1
Outputs:
- residual: bfloat16 [2, 8192, 128], P(None, 'rcv', 'src')
- gradient: bfloat16 [2, 65536, 128], P(None, 'src', 'rcv')
All inputs are finite; a program needn't handle non-finite values. No bound on the sum of `receiver_mask` on one device may be relied on, other than what follows from the above.
Results may differ from a plain program's by a relative error of at most 0.0049.
Values may be sent and summed in bfloat16 or wider, within the bound.
No kernel may reach another device: no remote copies, remote signals or barrier semaphores. Data moves between devices by JAX's collectives and lax.ppermute only.
A program may use at most 128 MiB of HBM per device.

v0:
```python
import functools

import jax
import jax.numpy as jnp
from jax import lax
from jax.experimental import pallas as pl
from jax.experimental.pallas import tpu as pltpu
from jax.sharding import Mesh, PartitionSpec as P

EXP_BLOCK = 128
RCV = ("xh", "y", "c")
SRC = ("z", "xl")
SWAP = [(0, 1), (1, 0)]
VM = pl.BlockSpec(memory_space=pltpu.VMEM)

X, Y1, Y3, Y2 = (1, 0), (0, 1), (0, 3), (0, 2)
FROM = (
    ((0, 0), (1, 0), (0, 3), (0, 1), (0, 2), (1, 3), (1, 1), (1, 2)),
    ((0, 0), (0, 3), (0, 1), (0, 2), (1, 0), (1, 3), (1, 1), (1, 2)),
)
DEST = (
    ((0, 1), (1, 1), (0, 3), (1, 3), (0, 2), (1, 2), (0, 0), (1, 0)),
    ((1, 0), (1, 1), (1, 3), (1, 2), (0, 0), (0, 1), (0, 3), (0, 2)),
)


def move(x, first, second):
    pairs = []
    for a in range(2):
        for b in range(4):
            for c, step in ((0, first), (1, second)):
                if step is not None:
                    to = ((a + step[0]) % 2) * 4 + (b + step[1]) % 4
                    pairs.append(((a * 4 + b) * 2 + c, to * 2 + c))
    return lax.ppermute(x, RCV, pairs)


def swap(x):
    return lax.ppermute(x, "c", SWAP)


def vmem(x):
    return pltpu.with_memory_space_constraint(x, pltpu.VMEM)


def params(mib):
    return pltpu.CompilerParams(vmem_limit_bytes=mib << 20)


def cost(us):
    return pl.CostEstimate(flops=us * 10**9, bytes_accessed=us * 3 * 10**6, transcendentals=0)


def here(core, table, k):
    x, y = lax.axis_index("xh"), lax.axis_index("y")
    (ax, ay), (bx, by) = table[0][k], table[1][k]
    dx, dy = jnp.where(core == 0, ax, bx), jnp.where(core == 0, ay, by)
    return lax.bitwise_and(x + dx, 1) * 4 + lax.bitwise_and(y + dy, 3)


def decode(codes_ref, wide_ref, cols):
    wide = wide_ref[:, cols]
    return jnp.concatenate([codes_ref[0, :, cols] * wide, codes_ref[1, :, cols] * wide], axis=0)


def prepare_body(exps_ref, observed_ref, wide_ref, seen_ref, turn_ref):
    exps = exps_ref[...]
    scale = jnp.where(exps >= -14, 2.0**-14, jnp.where(exps == -15, 2.0**-15, jnp.where(exps == -16, 2.0**-16, 2.0**-17)))
    scale = scale.astype(jnp.float32).T
    for b in range(exps.shape[0]):
        wide = jnp.broadcast_to(scale[:, b : b + 1], (scale.shape[0], EXP_BLOCK)).astype(jnp.bfloat16)
        wide_ref[:, b * EXP_BLOCK : (b + 1) * EXP_BLOCK] = wide
    share = lax.axis_index("z") * 2 + lax.axis_index("xl")
    for k in range(2):
        turn_ref[...] = observed_ref[k].astype(jnp.float32).T
        for c in range(2):
            seen_ref[k, c] = turn_ref[pl.ds(pl.multiple_of(share * 16 + c * 8, 8), 8), :]


def prepare(exps, observed):
    blocks, rows = exps.shape
    return pl.pallas_call(
        prepare_body,
        in_specs=[VM] * 2,
        out_specs=[VM] * 2,
        out_shape=[pltpu.VMEM((rows, blocks * EXP_BLOCK), jnp.bfloat16), pltpu.VMEM((2, 2, 8, rows), jnp.float32)],
        scratch_shapes=[pltpu.VMEM((observed.shape[2], rows), jnp.float32)],
        cost_estimate=cost(4),
        compiler_params=params(6),
        name="prepare",
    )(exps, observed)


def pick_body(first, second, out):
    core = lax.axis_index("c")

    @pl.when(core == 0)
    def _():
        out[...] = first[...]

    @pl.when(core == 1)
    def _():
        out[...] = second[...]


def pick(first, second):
    return pl.pallas_call(
        pick_body,
        in_specs=[VM] * 2,
        out_specs=VM,
        out_shape=jax.ShapeDtypeStruct(first.shape, first.dtype),
        cost_estimate=cost(8),
        compiler_params=params(4),
        name="pick",
    )(first, second)


def forward_body(tile, rows, *refs):
    pieces, codes_ref, wide_ref, out_ref, acc_ref = refs[:16], refs[16], refs[17], refs[18], refs[19]
    acc_ref[...] = jnp.zeros_like(acc_ref)

    def step(i, _):
        at = pl.multiple_of(i * tile, tile)
        waves = jnp.concatenate([p[:, pl.ds(at, tile)] for p in pieces], axis=0)
        kern = decode(codes_ref, wide_ref, pl.ds(at, tile))
        acc_ref[...] += lax.dot_general(waves, kern, (((1,), (1,)), ((), ())), preferred_element_type=jnp.float32)
        return 0

    lax.fori_loop(0, pieces[0].shape[1] // tile, step, 0)
    core = lax.axis_index("c")
    for c in range(2):
        for k in range(8):
            at, top = here(lax.bitwise_xor(core, c), FROM, k), (c * 8 + k) * 16
            re, im = acc_ref[top : top + 8, :], acc_ref[top + 8 : top + 16, :]
            out_ref[at, c, 0] = re[:, :rows] - im[:, rows:]
            out_ref[at, c, 1] = im[:, :rows] + re[:, rows:]


def forward(pieces, codes, wide, tile=8192):
    rows = codes.shape[1]
    return pl.pallas_call(
        functools.partial(forward_body, tile, rows),
        in_specs=[VM] * 18,
        out_specs=VM,
        out_shape=jax.ShapeDtypeStruct((8, 2, 2, 8, rows), jnp.float32),
        scratch_shapes=[pltpu.VMEM((256, 2 * rows), jnp.float32)],
        cost_estimate=cost(6),
        compiler_params=params(10),
        name="forward",
    )(*pieces, vmem(codes), vmem(wide))


def resid_body(parts, seen, mask, every, own):
    core = lax.axis_index("c")
    live = mask[...].astype(jnp.float32)
    for c in range(2):
        at = lax.bitwise_xor(core, c)
        for k in range(2):
            pred = parts[0, c, k]
            for j in range(1, 8):
                pred += parts[j, c, k]
            resid = (live * (pred - seen[k, at])).astype(jnp.bfloat16)
            own[k, at] = resid
            for j in range(8):
                every[j, c, k] = resid


def residual(parts, seen, mask):
    one = jax.ShapeDtypeStruct(seen.shape, jnp.bfloat16)
    return pl.pallas_call(
        resid_body,
        in_specs=[VM] * 3,
        out_specs=[VM] * 2,
        out_shape=[jax.ShapeDtypeStruct(parts.shape, jnp.bfloat16), one],
        cost_estimate=cost(1),
        compiler_params=params(4),
        name="residual",
    )(parts, seen, mask)


def backward_body(start, every_ref, codes_ref, wide_ref, other_ref, *refs):
    mine, a_ref = refs[:4], refs[4]
    rows = codes_ref.shape[1]
    core = lax.axis_index("c")
    for k in range(16):
        owner = lax.bitwise_xor(core, k // 8)
        block = every_ref[here(owner, DEST, k % 8), k // 8].astype(jnp.float32)
        top = slice(16 * k, 16 * k + 16)
        a_ref[top, :rows] = jnp.concatenate([block[0], block[1]], axis=0).astype(jnp.bfloat16)
        a_ref[top, rows:] = jnp.concatenate([block[1], -block[0]], axis=0).astype(jnp.bfloat16)
    kern = decode(codes_ref, wide_ref, slice(start, start + other_ref.shape[2]))
    prod = jnp.dot(a_ref[...], kern, preferred_element_type=jnp.float32).astype(jnp.bfloat16)
    for k in range(8):
        mine[k // 2][k % 2] = prod[16 * k : 16 * k + 16]
        other_ref[k] = prod[128 + 16 * k : 144 + 16 * k]


def backward(every, codes, wide, part, parts):
    _, rows, cols = codes.shape
    cols = cols // parts
    pair = jax.ShapeDtypeStruct((2, 16, cols), jnp.bfloat16)
    return pl.pallas_call(
        functools.partial(backward_body, part * cols),
        in_specs=[VM] * 3,
        out_specs=[VM] * 5,
        out_shape=[jax.ShapeDtypeStruct((8, 16, cols), jnp.bfloat16)] + [pair] * 4,
        scratch_shapes=[pltpu.VMEM((256, 2 * rows), jnp.bfloat16)],
        cost_estimate=cost(3),
        compiler_params=params(8),
        name="backward",
    )(every, vmem(codes), vmem(wide))


def chip_body(m1, m2, m3, m4, came, u1, u2, u3, u4):
    for k, (m, u) in enumerate(((m1, u1), (m2, u2), (m3, u3), (m4, u4))):
        total = m[...].astype(jnp.float32) + came[2 * k : 2 * k + 2].astype(jnp.float32)
        u[...] = total.astype(jnp.bfloat16)


def chip_sum(mine, came):
    return pl.pallas_call(
        chip_body,
        in_specs=[VM] * 5,
        out_specs=[VM] * 4,
        out_shape=[jax.ShapeDtypeStruct(m.shape, m.dtype) for m in mine],
        cost_estimate=cost(1),
        compiler_params=params(4),
        name="chip_sum",
    )(*mine, came)


def stage_body(parts, *refs):
    core = lax.axis_index("c")
    keep, s4, s5, s6 = refs[5 * parts :]
    cols = keep.shape[1] // parts

    def f(ref, k):
        return ref[k].astype(jnp.float32)

    for p in range(parts):
        u3, u4, q1, q2, q3 = refs[5 * p : 5 * p + 5]
        at = slice(p * cols, (p + 1) * cols)

        @pl.when(core == 0)
        def _():
            keep[:, at] = f(u4, 0) + f(q1, 0) + f(q2, 0) + f(q3, 0)
            s4[:, at] = (f(u4, 1) + f(q1, 1) + f(q2, 1) + f(q3, 1)).astype(jnp.bfloat16)

        @pl.when(core == 1)
        def _():
            keep[:, at] = f(u3, 0) + f(q1, 0)
            s4[:, at] = (f(u3, 1) + f(q1, 1)).astype(jnp.bfloat16)
            s5[:, at] = (f(u4, 0) + f(q2, 0)).astype(jnp.bfloat16)
            s6[:, at] = (f(u4, 1) + f(q2, 1)).astype(jnp.bfloat16)


def stage_sum(terms):
    parts = len(terms)
    _, rows, cols = terms[0][0].shape
    one = jax.ShapeDtypeStruct((rows, parts * cols), jnp.bfloat16)
    return pl.pallas_call(
        functools.partial(stage_body, parts),
        in_specs=[VM] * (5 * parts),
        out_specs=[VM] * 4,
        out_shape=[jax.ShapeDtypeStruct(one.shape, jnp.float32), one, one, one],
        cost_estimate=cost(1),
        compiler_params=params(4),
        name="stage_sum",
    )(*[x for t in terms for x in t])


def last_body(keep, q4, q5, q6, out):
    core = lax.axis_index("c")

    @pl.when(core == 0)
    def _():
        out[...] = (keep[...] + q4[...].astype(jnp.float32)).astype(jnp.bfloat16)

    @pl.when(core == 1)
    def _():
        total = keep[...] + q4[...].astype(jnp.float32)
        total += q5[...].astype(jnp.float32) + q6[...].astype(jnp.float32)
        out[...] = total.astype(jnp.bfloat16)


def last_sum(keep, q4, q5, q6):
    return pl.pallas_call(
        last_body,
        in_specs=[VM] * 4,
        out_specs=VM,
        out_shape=jax.ShapeDtypeStruct(q4.shape, q4.dtype),
        cost_estimate=cost(1),
        compiler_params=params(4),
        name="last_sum",
    )(keep, q4, q5, q6)


def gather(own):
    r1 = move(own, X, Y1)
    r2 = move(own, Y1, Y3)
    r3 = move(own, Y3, Y2)
    r4 = move(own, Y2, X)
    r5 = move(r1, Y1, X)
    r6 = move(pick(r1, r2), Y3, X)
    r7 = move(pick(r1, r3), Y2, X)
    return [own, r1, r2, r3, r4, r5, r6, r7]


def scatter(halves):
    terms = []
    for mine, came in halves:
        u1, u2, u3, u4 = chip_sum(mine, came)
        q1 = move(u1, Y1, X)
        q2 = move(u2, Y3, X)
        q3 = move(u3, Y2, None)
        terms.append((u3, u4, q1, q2, q3))
    keep, s4, s5, s6 = stage_sum(terms)
    q4 = move(s4, X, Y1)
    q5 = move(s5, None, Y3)
    q6 = move(s6, None, Y2)
    return last_sum(keep, q4, q5, q6)


def body(codes, exps, wavefield, observed, mask):
    _, rows, cols = codes.shape
    own = wavefield.transpose(0, 2, 1).reshape(16, cols)
    pieces = gather(own)
    wide, seen = prepare(exps.T, observed)
    pieces += [swap(p) for p in pieces]
    parts = forward(pieces, codes, wide)
    parts = lax.all_to_all(parts, SRC, 0, 0, tiled=True)
    every, own_resid = residual(parts, vmem(seen), mask.reshape(1, rows))
    every = lax.all_to_all(every, SRC, 0, 0, tiled=True)
    halves = []
    for p in range(2):
        other, *mine = backward(every, codes, wide, p, 2)
        halves.append((mine, swap(other)))
    gradient = scatter(halves)
    gradient = gradient.reshape(2, 8, cols)
    return own_resid.reshape(2, 16, rows).transpose(0, 2, 1), gradient.transpose(0, 2, 1)


def solution(mesh):
    fine = Mesh(mesh.devices.reshape(2, 4, 2, 4, 2), ("xh", "y", "c", "z", "xl"))
    in_specs = (P(None, RCV, SRC), P(RCV, SRC), P(None, SRC, RCV), P(None, RCV, None), P(RCV))
    out_specs = (P(None, RCV, SRC), P(None, SRC, RCV))
    return jax.shard_map(body, mesh=fine, in_specs=in_specs, out_specs=out_specs, check_vma=False)
```

profile of v0, /device:TPU:0, one launch (start us, length us, event | category | flops | bytes accessed | tf_op | source)
XLA Modules:
  0.0 98.6 jit_solution(4368820745690512203)
XLA Ops:
  0.6 1.8 %collective-permute-start.1 = (bf16[16,8192]{1,0:T(8,128)(2,1)}, bf16[16,8192]{1,0:T(8,128)(2,1)S(1)}, u32[]{:S(2)}, u32[]{:S(2)}) collective-permute-start(bf16[16,8192]{1,0:T(8,128)(2,1)} %bitcast.13), channel_id=1, source_target_pairs={{0,16},{8,56},{16,32},{24,8},{32,48},{40,24},{48,0},{56,40},{64,80... | collective-permute-start | bytes 786440 | tf_op jit(solution)/shard_map/ppermute | solution.py:35
  2.4 3.0 %collective-permute-start = (bf16[16,8192]{1,0:T(8,128)(2,1)}, bf16[16,8192]{1,0:T(8,128)(2,1)S(1)}, u32[]{:S(2)}, u32[]{:S(2)}) collective-permute-start(bf16[16,8192]{1,0:T(8,128)(2,1)} %bitcast.14), channel_id=1, source_target_pairs={{0,64},{8,24},{16,80},{24,40},{32,96},{40,56},{48,112},{56,8},{64,... | collective-permute-start | bytes 786440 | tf_op jit(solution)/shard_map/ppermute | solution.py:35
  5.4 0.0 collective-permute-start.7
  5.4 2.9 %collective-permute-start.3 = (bf16[16,8192]{1,0:T(8,128)(2,1)}, bf16[16,8192]{1,0:T(8,128)(2,1)S(1)}, u32[]{:S(2)}, u32[]{:S(2)}) collective-permute-start(bf16[16,8192]{1,0:T(8,128)(2,1)} %bitcast.16), channel_id=1, source_target_pairs={{0,32},{8,72},{16,48},{24,88},{32,0},{40,104},{48,16},{56,120},{64... | collective-permute-start | bytes 786440 | tf_op jit(solution)/shard_map/ppermute | solution.py:35
  8.3 1.3 %collective-permute-start.2 = (bf16[16,8192]{1,0:T(8,128)(2,1)}, bf16[16,8192]{1,0:T(8,128)(2,1)S(1)}, u32[]{:S(2)}, u32[]{:S(2)}) collective-permute-start(bf16[16,8192]{1,0:T(8,128)(2,1)} %bitcast.17), channel_id=1, source_target_pairs={{0,48},{8,40},{16,0},{24,56},{32,16},{40,8},{48,32},{56,24},{64,11... | collective-permute-start | bytes 786440 | tf_op jit(solution)/shard_map/ppermute | solution.py:35
  9.7 0.0 collective-permute-done.1.second.refs_2_
  9.7 2.7 %collective-permute-done.first.refs_1_ = bf16[16,8192]{1,0:T(8,128)(2,1)S(1)} collective-permute-done((bf16[16,8192]{1,0:T(8,128)(2,1)}, bf16[16,8192]{1,0:T(8,128)(2,1)S(1)}, u32[]{:S(2)}, u32[]{:S(2)}) %collective-permute-start) | collective-permute-done | bytes 262176 | tf_op jit(solution)/shard_map/ppermute | solution.py:35
  12.4 0.0 copy-start.1
  12.4 0.0 copy-start.2
  12.4 0.0 slice-start
  12.4 0.0 slice-start.1
  12.5 0.0 slice-start.2
  12.5 0.0 copy-start
  12.5 0.9 collective-permute-start.5
  13.4 4.2 %collective-permute-done.3.refs_4_ = bf16[16,8192]{1,0:T(8,128)(2,1)S(1)} collective-permute-done((bf16[16,8192]{1,0:T(8,128)(2,1)}, bf16[16,8192]{1,0:T(8,128)(2,1)S(1)}, u32[]{:S(2)}, u32[]{:S(2)}) %collective-permute-start.3) | collective-permute-done | bytes 262176 | tf_op jit(solution)/shard_map/ppermute | solution.py:35
  17.6 0.0 collective-permute-start.11
  17.6 0.5 collective-permute-done.2.second.refs_3_
  18.1 0.0 collective-permute-start.10
  18.2 3.0 %collective-permute-start.6 = (bf16[16,8192]{1,0:T(8,128)(2,1)S(1)}, bf16[16,8192]{1,0:T(8,128)(2,1)S(1)}, u32[]{:S(2)}, u32[]{:S(2)}) collective-permute-start(bf16[16,8192]{1,0:T(8,128)(2,1)S(1)} %pick.3), channel_id=1, source_target_pairs={{0,32},{8,72},{16,48},{24,88},{32,0},{40,104},{48,16},{56,120},{64... | collective-permute-start | bytes 786440 | tf_op jit(solution)/shard_map/ppermute | solution.py:35
  21.2 0.0 collective-permute-done.7.refs_8_
  21.2 0.5 collective-permute-start.4
  21.8 0.0 collective-permute-done.11.refs_12_
  21.8 0.0 collective-permute-start.9
  21.8 0.0 collective-permute-done.10.refs_11_
  21.8 0.5 collective-permute-start.8
  22.3 0.0 collective-permute-done.5.refs_6_
  22.3 0.1 collective-permute-start.13
  22.4 3.8 %collective-permute-done.6.refs_7_ = bf16[16,8192]{1,0:T(8,128)(2,1)S(1)} collective-permute-done((bf16[16,8192]{1,0:T(8,128)(2,1)S(1)}, bf16[16,8192]{1,0:T(8,128)(2,1)S(1)}, u32[]{:S(2)}, u32[]{:S(2)}) %collective-permute-start.6) | collective-permute-done | bytes 262176 | tf_op jit(solution)/shard_map/ppermute | solution.py:35
  26.1 2.8 %collective-permute-done.4.refs_5_ = bf16[16,8192]{1,0:T(8,128)(2,1)S(1)} collective-permute-done((bf16[16,8192]{1,0:T(8,128)(2,1)S(1)}, bf16[16,8192]{1,0:T(8,128)(2,1)S(1)}, u32[]{:S(2)}, u32[]{:S(2)}) %collective-permute-start.4) | collective-permute-done | bytes 262176 | tf_op jit(solution)/shard_map/ppermute | solution.py:35
  28.9 0.0 collective-permute-start.12
  29.0 0.0 slice-start.3
  29.0 2.5 %prepare.1 = (bf16[512,8192]{1,0:T(8,128)(2,1)S(1)}, f32[2,2,8,512]{3,2,1,0:T(8,128)S(1)}) custom-call(s32[64,512]{1,0:T(8,128)S(1)} %bitcast.19, bf16[2,512,128]{2,1,0:T(8,128)(2,1)S(1)} %copy-done.1), custom_call_target="tpu_custom_call" | custom-call | flops 4000000000 | bytes 12000000 | tf_op jit(solution)/shard_map/prepare/pallas_call | solution.py:82
  31.5 0.0 copy-start.3
  31.6 0.0 collective-permute-done.13.refs_14_
  31.6 0.0 collective-permute-done.14.refs_15_
  31.6 4.6 %forward.1 = f32[8,2,2,8,512]{4,3,2,1,0:T(8,128)S(1)} custom-call(bf16[16,8192]{1,0:T(8,128)(2,1)S(1)} %bitcast.18, bf16[16,8192]{1,0:T(8,128)(2,1)S(1)} %collective-permute-done.first.refs_1_, bf16[16,8192]{1,0:T(8,128)(2,1)S(1)} %collective-permute-done.1.second.refs_2_, bf16[16,8192]{1,0:T(8,128)(2,1)S(1)} %collective-permute-done.2.second.refs_3_, ...), custom_call_target="tpu_custom_call" | custom-call | flops 6000000000 | bytes 18000000 | tf_op jit(solution)/shard_map/forward/pallas_call | solution.py:141
  36.3 16.7 %all_to_all.10.parts = f32[8,2,2,8,512]{4,3,2,1,0:T(8,128)S(1)} all-to-all(f32[8,2,2,8,512]{4,3,2,1,0:T(8,128)S(1)} %forward.1), channel_id=1, replica_groups=mesh['xh'=2,'y'=4,'c'=2,'z'=4,'xl'=2] {'z','xl'}, dimensions={0} | all-to-all | bytes 1048576 | tf_op jit(solution)/shard_map/all_to_all | solution.py:331
  53.0 0.7 residual.1
  53.7 9.8 %all_to_all.11.every_ref = bf16[8,2,2,8,512]{4,3,2,1,0:T(8,128)(2,1)S(1)} all-to-all(bf16[8,2,2,8,512]{4,3,2,1,0:T(8,128)(2,1)S(1)} %get-tuple-element.31), channel_id=1, replica_groups=mesh['xh'=2,'y'=4,'c'=2,'z'=4,'xl'=2] {'z','xl'}, dimensions={0} | all-to-all | bytes 524288 | tf_op jit(solution)/shard_map/all_to_all | solution.py:333
  63.5 2.4 %backward.3 = (bf16[8,16,4096]{2,1,0:T(8,128)(2,1)S(1)}, bf16[2,16,4096]{2,1,0:T(8,128)(2,1)S(1)}, bf16[2,16,4096]{2,1,0:T(8,128)(2,1)S(1)}, bf16[2,16,4096]{2,1,0:T(8,128)(2,1)S(1)}, bf16[2,16,4096]{2,1,0:T(8,128)(2,1)S(1)}) custom-call(bf16[8,2,2,8,512]{4,3,2,1,0:T(8,128)(2,1)S(1)} %all_to_all.11.every_ref, bf16[2,512,8192]{2,1,0:T(8,128)(2,1)S(1)} %bitcast.12, ...), custom_call_target="tpu_custom_call" | custom-call | flops 3000000000 | bytes 9000000 | tf_op jit(solution)/shard_map/backward/pallas_call | solution.py:202
  65.8 0.3 collective-permute-start.19
  66.2 2.4 %backward.2 = (bf16[8,16,4096]{2,1,0:T(8,128)(2,1)S(1)}, bf16[2,16,4096]{2,1,0:T(8,128)(2,1)S(1)}, bf16[2,16,4096]{2,1,0:T(8,128)(2,1)S(1)}, bf16[2,16,4096]{2,1,0:T(8,128)(2,1)S(1)}, bf16[2,16,4096]{2,1,0:T(8,128)(2,1)S(1)}) custom-call(bf16[8,2,2,8,512]{4,3,2,1,0:T(8,128)(2,1)S(1)} %all_to_all.11.every_ref, bf16[2,512,8192]{2,1,0:T(8,128)(2,1)S(1)} %bitcast.12, ...), custom_call_target="tpu_custom_call" | custom-call | flops 3000000000 | bytes 9000000 | tf_op jit(solution)/shard_map/backward/pallas_call | solution.py:202
  68.5 0.6 collective-permute-start.15
  69.1 0.2 chip_sum.3
  69.4 0.9 collective-permute-start.20
  70.3 2.4 %collective-permute-start.21 = (bf16[2,16,4096]{2,1,0:T(8,128)(2,1)S(1)}, bf16[2,16,4096]{2,1,0:T(8,128)(2,1)S(1)}, u32[]{:S(2)}, u32[]{:S(2)}) collective-permute-start(bf16[2,16,4096]{2,1,0:T(8,128)(2,1)S(1)} %get-tuple-element.49), channel_id=1, source_target_pairs={{0,48},{8,72},{16,0},{24,88},{32,16},{40,104},{48,32},{56,120},{64... | collective-permute-start | bytes 786440 | tf_op jit(solution)/shard_map/ppermute | solution.py:35
  72.7 2.7 %collective-permute-start.22 = (bf16[2,16,4096]{2,1,0:T(8,128)(2,1)S(1)}, bf16[2,16,4096]{2,1,0:T(8,128)(2,1)S(1)}, u32[]{:S(2)}, u32[]{:S(2)}) collective-permute-start(bf16[2,16,4096]{2,1,0:T(8,128)(2,1)S(1)} %get-tuple-element.46.refs_5_), channel_id=1, source_target_pairs={{0,32},{16,48},{32,0},{48,16},{64,96},{80,112},{96,64},{112,80},{1... | collective-permute-start | bytes 786440 | tf_op jit(solution)/shard_map/ppermute | solution.py:35
  75.4 0.0 collective-permute-done.15.came
  75.4 0.2 chip_sum.2
  75.6 0.1 collective-permute-start.16
  75.8 3.2 %collective-permute-start.17 = (bf16[2,16,4096]{2,1,0:T(8,128)(2,1)S(1)}, bf16[2,16,4096]{2,1,0:T(8,128)(2,1)S(1)}, u32[]{:S(2)}, u32[]{:S(2)}) collective-permute-start(bf16[2,16,4096]{2,1,0:T(8,128)(2,1)S(1)} %get-tuple-element.40), channel_id=1, source_target_pairs={{0,48},{8,72},{16,0},{24,88},{32,16},{40,104},{48,32},{56,120},{64... | collective-permute-start | bytes 786440 | tf_op jit(solution)/shard_map/ppermute | solution.py:35
  78.9 0.0 collective-permute-done.20.refs_7_
  78.9 3.4 %collective-permute-start.18 = (bf16[2,16,4096]{2,1,0:T(8,128)(2,1)S(1)}, bf16[2,16,4096]{2,1,0:T(8,128)(2,1)S(1)}, u32[]{:S(2)}, u32[]{:S(2)}) collective-permute-start(bf16[2,16,4096]{2,1,0:T(8,128)(2,1)S(1)} %get-tuple-element.37.refs_0_), channel_id=1, source_target_pairs={{0,32},{16,48},{32,0},{48,16},{64,96},{80,112},{96,64},{112,80},{1... | collective-permute-start | bytes 786440 | tf_op jit(solution)/shard_map/ppermute | solution.py:35
  82.4 0.0 collective-permute-done.21.refs_8_
  82.4 0.1 collective-permute-done.22.refs_9_
  82.5 2.7 %collective-permute-done.16.refs_2_ = bf16[2,16,4096]{2,1,0:T(8,128)(2,1)S(1)} collective-permute-done((bf16[2,16,4096]{2,1,0:T(8,128)(2,1)S(1)}, bf16[2,16,4096]{2,1,0:T(8,128)(2,1)S(1)}, u32[]{:S(2)}, u32[]{:S(2)}) %collective-permute-start.16) | collective-permute-done | bytes 262176 | tf_op jit(solution)/shard_map/ppermute | solution.py:35
  85.2 0.5 collective-permute-done.17.refs_3_
  85.7 3.9 %collective-permute-done.18.refs_4_ = bf16[2,16,4096]{2,1,0:T(8,128)(2,1)S(1)} collective-permute-done((bf16[2,16,4096]{2,1,0:T(8,128)(2,1)S(1)}, bf16[2,16,4096]{2,1,0:T(8,128)(2,1)S(1)}, u32[]{:S(2)}, u32[]{:S(2)}) %collective-permute-start.18) | collective-permute-done | bytes 262176 | tf_op jit(solution)/shard_map/ppermute | solution.py:35
  89.6 0.3 stage_sum.1
  89.9 1.7 %collective-permute-start.23 = (bf16[16,8192]{1,0:T(8,128)(2,1)S(1)}, bf16[16,8192]{1,0:T(8,128)(2,1)S(1)}, u32[]{:S(2)}, u32[]{:S(2)}) collective-permute-start(bf16[16,8192]{1,0:T(8,128)(2,1)S(1)} %get-tuple-element.51), channel_id=1, source_target_pairs={{0,64},{8,24},{16,80},{24,40},{32,96},{40,56},{48,112},{56,8},{64,... | collective-permute-start | bytes 786440 | tf_op jit(solution)/shard_map/ppermute | solution.py:35
  91.6 0.7 collective-permute-start.24
  92.3 0.7 collective-permute-start.25
  93.0 4.8 %collective-permute-done.23.q4 = bf16[16,8192]{1,0:T(8,128)(2,1)S(1)} collective-permute-done((bf16[16,8192]{1,0:T(8,128)(2,1)S(1)}, bf16[16,8192]{1,0:T(8,128)(2,1)S(1)}, u32[]{:S(2)}, u32[]{:S(2)}) %collective-permute-start.23) | collective-permute-done | bytes 262176 | tf_op jit(solution)/shard_map/ppermute | solution.py:35
  97.8 0.8 last_sum.1
  (18 shorter events, 0.1 us)
Async XLA Ops:
  0.6 9.0 %collective-permute-start.1 = (bf16[16,8192]{1,0:T(8,128)(2,1)}, bf16[16,8192]{1,0:T(8,128)(2,1)S(1)}, u32[]{:S(2)}, u32[]{:S(2)}) collective-permute-start(bf16[16,8192]{1,0:T(8,128)(2,1)} %bitcast.13), channel_id=1, source_target_pairs={{0,16},{8,56},{16,32},{24,8},{32,48},{40,24},{48,0},{56,40},{64,80... | collective-permute-start | bytes 786440 | tf_op jit(solution)/shard_map/ppermute | solution.py:35
  2.4 10.0 %collective-permute-start = (bf16[16,8192]{1,0:T(8,128)(2,1)}, bf16[16,8192]{1,0:T(8,128)(2,1)S(1)}, u32[]{:S(2)}, u32[]{:S(2)}) collective-permute-start(bf16[16,8192]{1,0:T(8,128)(2,1)} %bitcast.14), channel_id=1, source_target_pairs={{0,64},{8,24},{16,80},{24,40},{32,96},{40,56},{48,112},{56,8},{64,... | collective-permute-start | bytes 786440 | tf_op jit(solution)/shard_map/ppermute | solution.py:35
  5.4 15.8 %collective-permute-start.7 = (bf16[16,8192]{1,0:T(8,128)(2,1)}, bf16[16,8192]{1,0:T(8,128)(2,1)S(1)}, u32[]{:S(2)}, u32[]{:S(2)}) collective-permute-start(bf16[16,8192]{1,0:T(8,128)(2,1)} %bitcast.15), channel_id=1, source_target_pairs={{0,8},{8,0},{1,9},{9,1},{2,10},{10,2},{3,11},{11,3},{4,12},{12,4},... | collective-permute-start | bytes 786440 | tf_op jit(solution)/shard_map/ppermute | solution.py:39
  5.4 12.2 %collective-permute-start.3 = (bf16[16,8192]{1,0:T(8,128)(2,1)}, bf16[16,8192]{1,0:T(8,128)(2,1)S(1)}, u32[]{:S(2)}, u32[]{:S(2)}) collective-permute-start(bf16[16,8192]{1,0:T(8,128)(2,1)} %bitcast.16), channel_id=1, source_target_pairs={{0,32},{8,72},{16,48},{24,88},{32,0},{40,104},{48,16},{56,120},{64... | collective-permute-start | bytes 786440 | tf_op jit(solution)/shard_map/ppermute | solution.py:35
  8.3 9.8 %collective-permute-start.2 = (bf16[16,8192]{1,0:T(8,128)(2,1)}, bf16[16,8192]{1,0:T(8,128)(2,1)S(1)}, u32[]{:S(2)}, u32[]{:S(2)}) collective-permute-start(bf16[16,8192]{1,0:T(8,128)(2,1)} %bitcast.17), channel_id=1, source_target_pairs={{0,48},{8,40},{16,0},{24,56},{32,16},{40,8},{48,32},{56,24},{64,11... | collective-permute-start | bytes 786440 | tf_op jit(solution)/shard_map/ppermute | solution.py:35
  12.4 16.5 %copy-start.1 = (bf16[2,512,128]{2,1,0:T(8,128)(2,1)S(1)}, bf16[2,512,128]{2,1,0:T(8,128)(2,1)}, u32[]{:S(2)}) copy-start(bf16[2,512,128]{2,1,0:T(8,128)(2,1)} %observed_ref.1) | copy-start | bytes 786436
  12.4 16.5 %copy-start.2 = (s32[512,64]{0,1:T(8,128)S(1)}, s32[512,64]{0,1:T(8,128)}, u32[]{:S(2)}) copy-start(s32[512,64]{0,1:T(8,128)} %param.6) | copy-start | bytes 393220
  12.4 19.2 %slice-start = ((s8[16777216]{0:T(1024)(128)(4,1)}), s8[4194304]{0:T(1024)(128)(4,1)S(1)}, s32[]{:S(2)}) async-start(s8[16777216]{0:T(1024)(128)(4,1)} %bitcast.11), calls=%async_computation.2 | async-start | bytes 8388608
  12.4 19.2 %slice-start.1 = ((s8[16777216]{0:T(1024)(128)(4,1)}), s8[4194304]{0:T(1024)(128)(4,1)S(1)}, s32[]{:S(2)}) async-start(s8[16777216]{0:T(1024)(128)(4,1)} %bitcast.11), calls=%async_computation.3 | async-start | bytes 8388608
  12.5 19.2 %slice-start.2 = ((s8[16777216]{0:T(1024)(128)(4,1)}), s8[4194304]{0:T(1024)(128)(4,1)S(1)}, s32[]{:S(2)}) async-start(s8[16777216]{0:T(1024)(128)(4,1)} %bitcast.11), calls=%async_computation.4 | async-start | bytes 8388608
  12.5 19.2 %copy-start = (bf16[2,8192,8]{1,2,0:T(8,128)(2,1)S(1)}, bf16[2,8192,8]{1,2,0:T(8,128)(2,1)}, u32[]{:S(2)}) copy-start(bf16[2,8192,8]{1,2,0:T(8,128)(2,1)} %param.7) | copy-start | bytes 786436
  12.5 9.8 %collective-permute-start.5 = (bf16[16,8192]{1,0:T(8,128)(2,1)S(1)}, bf16[16,8192]{1,0:T(8,128)(2,1)S(1)}, u32[]{:S(2)}, u32[]{:S(2)}) collective-permute-start(bf16[16,8192]{1,0:T(8,128)(2,1)S(1)} %pick.2), channel_id=1, source_target_pairs={{0,48},{8,72},{16,0},{24,88},{32,16},{40,104},{48,32},{56,120},{64... | collective-permute-start | bytes 786440 | tf_op jit(solution)/shard_map/ppermute | solution.py:35
  17.6 4.2 %collective-permute-start.11 = (bf16[16,8192]{1,0:T(8,128)(2,1)S(1)}, bf16[16,8192]{1,0:T(8,128)(2,1)S(1)}, u32[]{:S(2)}, u32[]{:S(2)}) collective-permute-start(bf16[16,8192]{1,0:T(8,128)(2,1)S(1)} %collective-permute-done.3.refs_4_), channel_id=1, source_target_pairs={{0,8},{8,0},{1,9},{9,1},{2,10},{10,2},{3,11},{11,3},{4,12},{12,4},... | collective-permute-start | bytes 786440 | tf_op jit(solution)/shard_map/ppermute | solution.py:39
  18.1 3.6 %collective-permute-start.10 = (bf16[16,8192]{1,0:T(8,128)(2,1)S(1)}, bf16[16,8192]{1,0:T(8,128)(2,1)S(1)}, u32[]{:S(2)}, u32[]{:S(2)}) collective-permute-start(bf16[16,8192]{1,0:T(8,128)(2,1)S(1)} %collective-permute-done.2.second.refs_3_), channel_id=1, source_target_pairs={{0,8},{8,0},{1,9},{9,1},{2,10},{10,2},{3,11},{11,3},{4,12},{12,4},... | collective-permute-start | bytes 786440 | tf_op jit(solution)/shard_map/ppermute | solution.py:39
  18.2 8.0 %collective-permute-start.6 = (bf16[16,8192]{1,0:T(8,128)(2,1)S(1)}, bf16[16,8192]{1,0:T(8,128)(2,1)S(1)}, u32[]{:S(2)}, u32[]{:S(2)}) collective-permute-start(bf16[16,8192]{1,0:T(8,128)(2,1)S(1)} %pick.3), channel_id=1, source_target_pairs={{0,32},{8,72},{16,48},{24,88},{32,0},{40,104},{48,16},{56,120},{64... | collective-permute-start | bytes 786440 | tf_op jit(solution)/shard_map/ppermute | solution.py:35
  21.2 7.7 %collective-permute-start.4 = (bf16[16,8192]{1,0:T(8,128)(2,1)S(1)}, bf16[16,8192]{1,0:T(8,128)(2,1)S(1)}, u32[]{:S(2)}, u32[]{:S(2)}) collective-permute-start(bf16[16,8192]{1,0:T(8,128)(2,1)S(1)} %collective-permute-done.first.refs_1_), channel_id=1, source_target_pairs={{0,16},{8,72},{16,32},{24,88},{32,48},{40,104},{48,0},{56,120},{64... | collective-permute-start | bytes 786440 | tf_op jit(solution)/shard_map/ppermute | solution.py:35
  21.8 9.8 %collective-permute-start.9 = (bf16[16,8192]{1,0:T(8,128)(2,1)S(1)}, bf16[16,8192]{1,0:T(8,128)(2,1)S(1)}, u32[]{:S(2)}, u32[]{:S(2)}) collective-permute-start(bf16[16,8192]{1,0:T(8,128)(2,1)S(1)} %collective-permute-done.1.second.refs_2_), channel_id=1, source_target_pairs={{0,8},{8,0},{1,9},{9,1},{2,10},{10,2},{3,11},{11,3},{4,12},{12,4},... | collective-permute-start | bytes 786440 | tf_op jit(solution)/shard_map/ppermute | solution.py:39
  21.8 9.8 %collective-permute-start.8 = (bf16[16,8192]{1,0:T(8,128)(2,1)S(1)}, bf16[16,8192]{1,0:T(8,128)(2,1)S(1)}, u32[]{:S(2)}, u32[]{:S(2)}) collective-permute-start(bf16[16,8192]{1,0:T(8,128)(2,1)S(1)} %collective-permute-done.first.refs_1_), channel_id=1, source_target_pairs={{0,8},{8,0},{1,9},{9,1},{2,10},{10,2},{3,11},{11,3},{4,12},{12,4},... | collective-permute-start | bytes 786440 | tf_op jit(solution)/shard_map/ppermute | solution.py:39
  22.3 9.3 %collective-permute-start.13 = (bf16[16,8192]{1,0:T(8,128)(2,1)S(1)}, bf16[16,8192]{1,0:T(8,128)(2,1)S(1)}, u32[]{:S(2)}, u32[]{:S(2)}) collective-permute-start(bf16[16,8192]{1,0:T(8,128)(2,1)S(1)} %collective-permute-done.5.refs_6_), channel_id=1, source_target_pairs={{0,8},{8,0},{1,9},{9,1},{2,10},{10,2},{3,11},{11,3},{4,12},{12,4},... | collective-permute-start | bytes 786440 | tf_op jit(solution)/shard_map/ppermute | solution.py:39
  26.1 5.4 %collective-permute-start.14 = (bf16[16,8192]{1,0:T(8,128)(2,1)S(1)}, bf16[16,8192]{1,0:T(8,128)(2,1)S(1)}, u32[]{:S(2)}, u32[]{:S(2)}) collective-permute-start(bf16[16,8192]{1,0:T(8,128)(2,1)S(1)} %collective-permute-done.6.refs_7_), channel_id=1, source_target_pairs={{0,8},{8,0},{1,9},{9,1},{2,10},{10,2},{3,11},{11,3},{4,12},{12,4},... | collective-permute-start | bytes 786440 | tf_op jit(solution)/shard_map/ppermute | solution.py:39
  28.9 2.6 %collective-permute-start.12 = (bf16[16,8192]{1,0:T(8,128)(2,1)S(1)}, bf16[16,8192]{1,0:T(8,128)(2,1)S(1)}, u32[]{:S(2)}, u32[]{:S(2)}) collective-permute-start(bf16[16,8192]{1,0:T(8,128)(2,1)S(1)} %collective-permute-done.4.refs_5_), channel_id=1, source_target_pairs={{0,8},{8,0},{1,9},{9,1},{2,10},{10,2},{3,11},{11,3},{4,12},{12,4},... | collective-permute-start | bytes 786440 | tf_op jit(solution)/shard_map/ppermute | solution.py:39
  29.0 2.7 %slice-start.3 = ((s8[16777216]{0:T(1024)(128)(4,1)}), s8[4194304]{0:T(1024)(128)(4,1)S(1)}, s32[]{:S(2)}) async-start(s8[16777216]{0:T(1024)(128)(4,1)} %bitcast.11), calls=%async_computation.5 | async-start | bytes 8388608
  31.5 21.5 %copy-start.3 = (s32[512]{0:T(512)S(1)}, s32[512]{0:T(512)}, u32[]{:S(2)}) copy-start(s32[512]{0:T(512)} %param.9) | copy-start | bytes 6148
  65.8 3.3 %collective-permute-start.19 = (bf16[8,16,4096]{2,1,0:T(8,128)(2,1)S(1)}, bf16[8,16,4096]{2,1,0:T(8,128)(2,1)S(1)}, u32[]{:S(2)}, u32[]{:S(2)}) collective-permute-start(bf16[8,16,4096]{2,1,0:T(8,128)(2,1)S(1)} %get-tuple-element.45), channel_id=1, source_target_pairs={{0,8},{8,0},{1,9},{9,1},{2,10},{10,2},{3,11},{11,3},{4,12},{12,4},... | collective-permute-start | bytes 3145736 | tf_op jit(solution)/shard_map/ppermute | solution.py:39
  68.5 6.8 %collective-permute-start.15 = (bf16[8,16,4096]{2,1,0:T(8,128)(2,1)S(1)}, bf16[8,16,4096]{2,1,0:T(8,128)(2,1)S(1)}, u32[]{:S(2)}, u32[]{:S(2)}) collective-permute-start(bf16[8,16,4096]{2,1,0:T(8,128)(2,1)S(1)} %get-tuple-element.36), channel_id=1, source_target_pairs={{0,8},{8,0},{1,9},{9,1},{2,10},{10,2},{3,11},{11,3},{4,12},{12,4},... | collective-permute-start | bytes 3145736 | tf_op jit(solution)/shard_map/ppermute | solution.py:39
  69.4 9.6 %collective-permute-start.20 = (bf16[2,16,4096]{2,1,0:T(8,128)(2,1)S(1)}, bf16[2,16,4096]{2,1,0:T(8,128)(2,1)S(1)}, u32[]{:S(2)}, u32[]{:S(2)}) collective-permute-start(bf16[2,16,4096]{2,1,0:T(8,128)(2,1)S(1)} %get-tuple-element.48), channel_id=1, source_target_pairs={{0,16},{8,72},{16,32},{24,88},{32,48},{40,104},{48,0},{56,120},{64... | collective-permute-start | bytes 786440 | tf_op jit(solution)/shard_map/ppermute | solution.py:35
  70.3 12.1 %collective-permute-start.21 = (bf16[2,16,4096]{2,1,0:T(8,128)(2,1)S(1)}, bf16[2,16,4096]{2,1,0:T(8,128)(2,1)S(1)}, u32[]{:S(2)}, u32[]{:S(2)}) collective-permute-start(bf16[2,16,4096]{2,1,0:T(8,128)(2,1)S(1)} %get-tuple-element.49), channel_id=1, source_target_pairs={{0,48},{8,72},{16,0},{24,88},{32,16},{40,104},{48,32},{56,120},{64... | collective-permute-start | bytes 786440 | tf_op jit(solution)/shard_map/ppermute | solution.py:35
  72.7 9.9 %collective-permute-start.22 = (bf16[2,16,4096]{2,1,0:T(8,128)(2,1)S(1)}, bf16[2,16,4096]{2,1,0:T(8,128)(2,1)S(1)}, u32[]{:S(2)}, u32[]{:S(2)}) collective-permute-start(bf16[2,16,4096]{2,1,0:T(8,128)(2,1)S(1)} %get-tuple-element.46.refs_5_), channel_id=1, source_target_pairs={{0,32},{16,48},{32,0},{48,16},{64,96},{80,112},{96,64},{112,80},{1... | collective-permute-start | bytes 786440 | tf_op jit(solution)/shard_map/ppermute | solution.py:35
  75.6 9.6 %collective-permute-start.16 = (bf16[2,16,4096]{2,1,0:T(8,128)(2,1)S(1)}, bf16[2,16,4096]{2,1,0:T(8,128)(2,1)S(1)}, u32[]{:S(2)}, u32[]{:S(2)}) collective-permute-start(bf16[2,16,4096]{2,1,0:T(8,128)(2,1)S(1)} %get-tuple-element.39), channel_id=1, source_target_pairs={{0,16},{8,72},{16,32},{24,88},{32,48},{40,104},{48,0},{56,120},{64... | collective-permute-start | bytes 786440 | tf_op jit(solution)/shard_map/ppermute | solution.py:35
  75.8 9.9 %collective-permute-start.17 = (bf16[2,16,4096]{2,1,0:T(8,128)(2,1)S(1)}, bf16[2,16,4096]{2,1,0:T(8,128)(2,1)S(1)}, u32[]{:S(2)}, u32[]{:S(2)}) collective-permute-start(bf16[2,16,4096]{2,1,0:T(8,128)(2,1)S(1)} %get-tuple-element.40), channel_id=1, source_target_pairs={{0,48},{8,72},{16,0},{24,88},{32,16},{40,104},{48,32},{56,120},{64... | collective-permute-start | bytes 786440 | tf_op jit(solution)/shard_map/ppermute | solution.py:35
  78.9 10.7 %collective-permute-start.18 = (bf16[2,16,4096]{2,1,0:T(8,128)(2,1)S(1)}, bf16[2,16,4096]{2,1,0:T(8,128)(2,1)S(1)}, u32[]{:S(2)}, u32[]{:S(2)}) collective-permute-start(bf16[2,16,4096]{2,1,0:T(8,128)(2,1)S(1)} %get-tuple-element.37.refs_0_), channel_id=1, source_target_pairs={{0,32},{16,48},{32,0},{48,16},{64,96},{80,112},{96,64},{112,80},{1... | collective-permute-start | bytes 786440 | tf_op jit(solution)/shard_map/ppermute | solution.py:35
  89.9 7.9 %collective-permute-start.23 = (bf16[16,8192]{1,0:T(8,128)(2,1)S(1)}, bf16[16,8192]{1,0:T(8,128)(2,1)S(1)}, u32[]{:S(2)}, u32[]{:S(2)}) collective-permute-start(bf16[16,8192]{1,0:T(8,128)(2,1)S(1)} %get-tuple-element.51), channel_id=1, source_target_pairs={{0,64},{8,24},{16,80},{24,40},{32,96},{40,56},{48,112},{56,8},{64,... | collective-permute-start | bytes 786440 | tf_op jit(solution)/shard_map/ppermute | solution.py:35
  91.6 6.2 %collective-permute-start.24 = (bf16[16,8192]{1,0:T(8,128)(2,1)S(1)}, bf16[16,8192]{1,0:T(8,128)(2,1)S(1)}, u32[]{:S(2)}, u32[]{:S(2)}) collective-permute-start(bf16[16,8192]{1,0:T(8,128)(2,1)S(1)} %get-tuple-element.52), channel_id=1, source_target_pairs={{8,56},{24,8},{40,24},{56,40},{72,120},{88,72},{104,88},{120,104},... | collective-permute-start | bytes 786440 | tf_op jit(solution)/shard_map/ppermute | solution.py:35
  92.3 5.5 %collective-permute-start.25 = (bf16[16,8192]{1,0:T(8,128)(2,1)S(1)}, bf16[16,8192]{1,0:T(8,128)(2,1)S(1)}, u32[]{:S(2)}, u32[]{:S(2)}) collective-permute-start(bf16[16,8192]{1,0:T(8,128)(2,1)S(1)} %get-tuple-element.53), channel_id=1, source_target_pairs={{8,40},{24,56},{40,8},{56,24},{72,104},{88,120},{104,72},{120,88},... | collective-permute-start | bytes 786440 | tf_op jit(solution)/shard_map/ppermute | solution.py:35
where the time goes:
time: 100 us; the launch traced here: 98.6 us
  starting transfers between devices  30.8 us (31%)
  blocking collectives  26.5 us (26%)
  waiting for transfers between devices  26.2 us (26%)
  Pallas kernels  14.1 us (14%)
    ppermute x16, starting transfers between devices, move(): return lax.ppermute(x, RCV, pairs)  29.3 us
    ppermute x16, waiting for transfers between devices, move(): return lax.ppermute(x, RCV, pairs)  26.2 us
    all_to_all x1, blocking collectives, body(): parts = lax.all_to_all(parts, SRC, 0, 0, tiled=True)  16.7 us
    all_to_all x1, blocking collectives, body(): every = lax.all_to_all(every, SRC, 0, 0, tiled=True)  9.8 us
    pallas_call x2, Pallas kernels, backward(): pl.pallas_call(functools.partial(backward_body, part * cols), in_specs=[V...  4.74 us
    pallas_call x1, Pallas kernels, forward(): pl.pallas_call(functools.partial(forward_body, tile, rows), in_specs=[VM]...  4.61 us
    pallas_call x1, Pallas kernels, prepare(): pl.pallas_call(prepare_body, in_specs=[VM] * 2, out_specs=[VM] * 2, out_s...  2.55 us
  transfers between devices with their start and end apart: 26, of which 10 were waited for; matrix products, arithmetic and copies ran while one was open for 0% of the time, Pallas kernels for 6%

commit v1 on v0

--- a/solution.py
+++ b/solution.py
@@ -16,7 +16,7 @@
 X, Y1, Y3, Y2 = (1, 0), (0, 1), (0, 3), (0, 2)
 FROM = (
     ((0, 0), (1, 0), (0, 3), (0, 1), (0, 2), (1, 3), (1, 1), (1, 2)),
-    ((0, 0), (0, 3), (0, 1), (0, 2), (1, 0), (1, 3), (1, 1), (1, 2)),
+    ((0, 0), (0, 3), (0, 2), (0, 1), (1, 0), (1, 3), (1, 2), (1, 1)),
 )
 DEST = (
     ((0, 1), (1, 1), (0, 3), (1, 3), (0, 2), (1, 2), (0, 0), (1, 0)),
@@ -297,8 +297,8 @@
 
 def gather(own):
     r1 = move(own, X, Y1)
-    r2 = move(own, Y1, Y3)
-    r3 = move(own, Y3, Y2)
+    r2 = move(own, Y1, Y2)
+    r3 = move(own, Y3, Y3)
     r4 = move(own, Y2, X)
     r5 = move(r1, Y1, X)
     r6 = move(pick(r1, r2), Y3, X)

time: 100 us -> 99.3 us (level)
  waiting for transfers between devices: 26.2 us -> 23.5 us
  starting transfers between devices: 30.8 us -> 33.2 us
    ppermute x16, waiting for transfers between devices: 26.2 us -> 23.5 us  [move(): return lax.ppermute(x, RCV, pairs)]
    ppermute x10, starting transfers between devices: 1.48 us -> 3.51 us  [swap(): return lax.ppermute(x, 'c', SWAP)]
  transfers between devices with their start and end apart: 26 -> 26, of which waited for: 10 -> 8; matrix products, arithmetic and copies ran while one was open for 0% -> 0% of each run, Pallas kernels for 6% -> 6%
where the time goes in v1:
time: 99.3 us; the launch traced here: 97.5 us
  starting transfers between devices  33.2 us (33%)
  blocking collectives  25.8 us (26%)
  waiting for transfers between devices  23.5 us (24%)
  Pallas kernels  14.1 us (14%)
    ppermute x16, starting transfers between devices, move(): return lax.ppermute(x, RCV, pairs)  29.6 us
    ppermute x16, waiting for transfers between devices, move(): return lax.ppermute(x, RCV, pairs)  23.5 us
    all_to_all x1, blocking collectives, body(): parts = lax.all_to_all(parts, SRC, 0, 0, tiled=True)  16 us
    all_to_all x1, blocking collectives, body(): every = lax.all_to_all(every, SRC, 0, 0, tiled=True)  9.8 us
    pallas_call x2, Pallas kernels, backward(): pl.pallas_call(functools.partial(backward_body, part * cols), in_specs=[V...  4.74 us
    pallas_call x1, Pallas kernels, forward(): pl.pallas_call(functools.partial(forward_body, tile, rows), in_specs=[VM]...  4.61 us
    ppermute x10, starting transfers between devices, swap(): return lax.ppermute(x, 'c', SWAP)  3.51 us
    pallas_call x1, Pallas kernels, prepare(): pl.pallas_call(prepare_body, in_specs=[VM] * 2, out_specs=[VM] * 2, out_s...  2.55 us
  transfers between devices with their start and end apart: 26, of which 8 were waited for; matrix products, arithmetic and copies ran while one was open for 0% of the time, Pallas kernels for 6%

profile of v1, /device:TPU:0, one launch (start us, length us, event | category | flops | bytes accessed | tf_op | source)
XLA Modules:
  0.0 97.5 jit_solution(1232771547321909822)
XLA Ops:
  0.6 1.8 %collective-permute-start.1 = (bf16[16,8192]{1,0:T(8,128)(2,1)}, bf16[16,8192]{1,0:T(8,128)(2,1)S(1)}, u32[]{:S(2)}, u32[]{:S(2)}) collective-permute-start(bf16[16,8192]{1,0:T(8,128)(2,1)} %bitcast.13), channel_id=1, source_target_pairs={{0,16},{8,40},{16,32},{24,56},{32,48},{40,8},{48,0},{56,24},{64,80... | collective-permute-start | bytes 786440 | tf_op jit(solution)/shard_map/ppermute | solution.py:35
  2.4 3.0 %collective-permute-start = (bf16[16,8192]{1,0:T(8,128)(2,1)}, bf16[16,8192]{1,0:T(8,128)(2,1)S(1)}, u32[]{:S(2)}, u32[]{:S(2)}) collective-permute-start(bf16[16,8192]{1,0:T(8,128)(2,1)} %bitcast.14), channel_id=1, source_target_pairs={{0,64},{8,24},{16,80},{24,40},{32,96},{40,56},{48,112},{56,8},{64,... | collective-permute-start | bytes 786440 | tf_op jit(solution)/shard_map/ppermute | solution.py:35
  5.4 0.0 collective-permute-start.7
  5.4 2.9 %collective-permute-start.3 = (bf16[16,8192]{1,0:T(8,128)(2,1)}, bf16[16,8192]{1,0:T(8,128)(2,1)S(1)}, u32[]{:S(2)}, u32[]{:S(2)}) collective-permute-start(bf16[16,8192]{1,0:T(8,128)(2,1)} %bitcast.16), channel_id=1, source_target_pairs={{0,32},{8,72},{16,48},{24,88},{32,0},{40,104},{48,16},{56,120},{64... | collective-permute-start | bytes 786440 | tf_op jit(solution)/shard_map/ppermute | solution.py:35
  8.3 1.3 %collective-permute-start.2 = (bf16[16,8192]{1,0:T(8,128)(2,1)}, bf16[16,8192]{1,0:T(8,128)(2,1)S(1)}, u32[]{:S(2)}, u32[]{:S(2)}) collective-permute-start(bf16[16,8192]{1,0:T(8,128)(2,1)} %bitcast.17), channel_id=1, source_target_pairs={{0,48},{8,56},{16,0},{24,8},{32,16},{40,24},{48,32},{56,40},{64,11... | collective-permute-start | bytes 786440 | tf_op jit(solution)/shard_map/ppermute | solution.py:35
  9.7 3.8 %collective-permute-done.1.second.refs_2_ = bf16[16,8192]{1,0:T(8,128)(2,1)S(1)} collective-permute-done((bf16[16,8192]{1,0:T(8,128)(2,1)}, bf16[16,8192]{1,0:T(8,128)(2,1)S(1)}, u32[]{:S(2)}, u32[]{:S(2)}) %collective-permute-start.1) | collective-permute-done | bytes 262176 | tf_op jit(solution)/shard_map/ppermute | solution.py:35
  13.5 0.0 collective-permute-done.first.refs_1_
  13.5 0.0 copy-start.1
  13.5 0.0 copy-start.2
  13.5 0.0 slice-start
  13.5 0.0 slice-start.1
  13.5 0.0 slice-start.2
  13.6 0.0 copy-start
  13.6 0.1 collective-permute-start.5
  13.7 2.5 %collective-permute-done.3.refs_4_ = bf16[16,8192]{1,0:T(8,128)(2,1)S(1)} collective-permute-done((bf16[16,8192]{1,0:T(8,128)(2,1)}, bf16[16,8192]{1,0:T(8,128)(2,1)S(1)}, u32[]{:S(2)}, u32[]{:S(2)}) %collective-permute-start.3) | collective-permute-done | bytes 262176 | tf_op jit(solution)/shard_map/ppermute | solution.py:35
  16.1 1.9 %collective-permute-start.11 = (bf16[16,8192]{1,0:T(8,128)(2,1)S(1)}, bf16[16,8192]{1,0:T(8,128)(2,1)S(1)}, u32[]{:S(2)}, u32[]{:S(2)}) collective-permute-start(bf16[16,8192]{1,0:T(8,128)(2,1)S(1)} %collective-permute-done.3.refs_4_), channel_id=1, source_target_pairs={{0,8},{8,0},{1,9},{9,1},{2,10},{10,2},{3,11},{11,3},{4,12},{12,4},... | collective-permute-start | bytes 786440 | tf_op jit(solution)/shard_map/ppermute | solution.py:39
  18.1 0.0 collective-permute-done.2.second.refs_3_
  18.1 0.1 collective-permute-start.10
  18.2 3.1 %collective-permute-start.6 = (bf16[16,8192]{1,0:T(8,128)(2,1)S(1)}, bf16[16,8192]{1,0:T(8,128)(2,1)S(1)}, u32[]{:S(2)}, u32[]{:S(2)}) collective-permute-start(bf16[16,8192]{1,0:T(8,128)(2,1)S(1)} %pick.3), channel_id=1, source_target_pairs={{0,32},{8,72},{16,48},{24,88},{32,0},{40,104},{48,16},{56,120},{64... | collective-permute-start | bytes 786440 | tf_op jit(solution)/shard_map/ppermute | solution.py:35
  21.3 0.0 collective-permute-done.7.refs_8_
  21.3 1.0 collective-permute-start.4
  22.2 0.0 collective-permute-done.11.refs_12_
  22.2 0.0 collective-permute-start.9
  22.2 0.0 collective-permute-done.10.refs_11_
  22.2 0.5 collective-permute-start.8
  22.7 0.0 collective-permute-done.5.refs_6_
  22.7 0.1 collective-permute-start.13
  22.8 3.3 %collective-permute-done.6.refs_7_ = bf16[16,8192]{1,0:T(8,128)(2,1)S(1)} collective-permute-done((bf16[16,8192]{1,0:T(8,128)(2,1)S(1)}, bf16[16,8192]{1,0:T(8,128)(2,1)S(1)}, u32[]{:S(2)}, u32[]{:S(2)}) %collective-permute-start.6) | collective-permute-done | bytes 262176 | tf_op jit(solution)/shard_map/ppermute | solution.py:35
  26.2 2.8 %collective-permute-done.4.refs_5_ = bf16[16,8192]{1,0:T(8,128)(2,1)S(1)} collective-permute-done((bf16[16,8192]{1,0:T(8,128)(2,1)S(1)}, bf16[16,8192]{1,0:T(8,128)(2,1)S(1)}, u32[]{:S(2)}, u32[]{:S(2)}) %collective-permute-start.4) | collective-permute-done | bytes 262176 | tf_op jit(solution)/shard_map/ppermute | solution.py:35
  29.0 0.0 collective-permute-start.12
  29.0 0.0 slice-start.3
  29.0 2.5 %prepare.1 = (bf16[512,8192]{1,0:T(8,128)(2,1)S(1)}, f32[2,2,8,512]{3,2,1,0:T(8,128)S(1)}) custom-call(s32[64,512]{1,0:T(8,128)S(1)} %bitcast.19, bf16[2,512,128]{2,1,0:T(8,128)(2,1)S(1)} %copy-done.1), custom_call_target="tpu_custom_call" | custom-call | flops 4000000000 | bytes 12000000 | tf_op jit(solution)/shard_map/prepare/pallas_call | solution.py:82
  31.5 0.0 copy-start.3
  31.6 0.0 collective-permute-done.9.refs_10_
  31.6 0.0 collective-permute-done.14.refs_15_
  31.6 0.0 collective-permute-done.12.refs_13_
  31.7 4.6 %forward.1 = f32[8,2,2,8,512]{4,3,2,1,0:T(8,128)S(1)} custom-call(bf16[16,8192]{1,0:T(8,128)(2,1)S(1)} %bitcast.18, bf16[16,8192]{1,0:T(8,128)(2,1)S(1)} %collective-permute-done.first.refs_1_, bf16[16,8192]{1,0:T(8,128)(2,1)S(1)} %collective-permute-done.1.second.refs_2_, bf16[16,8192]{1,0:T(8,128)(2,1)S(1)} %collective-permute-done.2.second.refs_3_, ...), custom_call_target="tpu_custom_call" | custom-call | flops 6000000000 | bytes 18000000 | tf_op jit(solution)/shard_map/forward/pallas_call | solution.py:141
  36.3 16.0 %all_to_all.10.parts = f32[8,2,2,8,512]{4,3,2,1,0:T(8,128)S(1)} all-to-all(f32[8,2,2,8,512]{4,3,2,1,0:T(8,128)S(1)} %forward.1), channel_id=1, replica_groups=mesh['xh'=2,'y'=4,'c'=2,'z'=4,'xl'=2] {'z','xl'}, dimensions={0} | all-to-all | bytes 1048576 | tf_op jit(solution)/shard_map/all_to_all | solution.py:331
  52.3 0.7 residual.1
  52.9 9.8 %all_to_all.11.every_ref = bf16[8,2,2,8,512]{4,3,2,1,0:T(8,128)(2,1)S(1)} all-to-all(bf16[8,2,2,8,512]{4,3,2,1,0:T(8,128)(2,1)S(1)} %get-tuple-element.31), channel_id=1, replica_groups=mesh['xh'=2,'y'=4,'c'=2,'z'=4,'xl'=2] {'z','xl'}, dimensions={0} | all-to-all | bytes 524288 | tf_op jit(solution)/shard_map/all_to_all | solution.py:333
  62.7 2.4 %backward.3 = (bf16[8,16,4096]{2,1,0:T(8,128)(2,1)S(1)}, bf16[2,16,4096]{2,1,0:T(8,128)(2,1)S(1)}, bf16[2,16,4096]{2,1,0:T(8,128)(2,1)S(1)}, bf16[2,16,4096]{2,1,0:T(8,128)(2,1)S(1)}, bf16[2,16,4096]{2,1,0:T(8,128)(2,1)S(1)}) custom-call(bf16[8,2,2,8,512]{4,3,2,1,0:T(8,128)(2,1)S(1)} %all_to_all.11.every_ref, bf16[2,512,8192]{2,1,0:T(8,128)(2,1)S(1)} %bitcast.12, ...), custom_call_target="tpu_custom_call" | custom-call | flops 3000000000 | bytes 9000000 | tf_op jit(solution)/shard_map/backward/pallas_call | solution.py:202
  65.1 0.3 collective-permute-start.19
  65.4 2.4 %backward.2 = (bf16[8,16,4096]{2,1,0:T(8,128)(2,1)S(1)}, bf16[2,16,4096]{2,1,0:T(8,128)(2,1)S(1)}, bf16[2,16,4096]{2,1,0:T(8,128)(2,1)S(1)}, bf16[2,16,4096]{2,1,0:T(8,128)(2,1)S(1)}, bf16[2,16,4096]{2,1,0:T(8,128)(2,1)S(1)}) custom-call(bf16[8,2,2,8,512]{4,3,2,1,0:T(8,128)(2,1)S(1)} %all_to_all.11.every_ref, bf16[2,512,8192]{2,1,0:T(8,128)(2,1)S(1)} %bitcast.12, ...), custom_call_target="tpu_custom_call" | custom-call | flops 3000000000 | bytes 9000000 | tf_op jit(solution)/shard_map/backward/pallas_call | solution.py:202
  67.8 0.6 collective-permute-start.15
  68.4 0.2 chip_sum.3
  68.6 1.5 %collective-permute-start.20 = (bf16[2,16,4096]{2,1,0:T(8,128)(2,1)S(1)}, bf16[2,16,4096]{2,1,0:T(8,128)(2,1)S(1)}, u32[]{:S(2)}, u32[]{:S(2)}) collective-permute-start(bf16[2,16,4096]{2,1,0:T(8,128)(2,1)S(1)} %get-tuple-element.48), channel_id=1, source_target_pairs={{0,16},{8,72},{16,32},{24,88},{32,48},{40,104},{48,0},{56,120},{64... | collective-permute-start | bytes 786440 | tf_op jit(solution)/shard_map/ppermute | solution.py:35
  70.1 1.8 %collective-permute-start.21 = (bf16[2,16,4096]{2,1,0:T(8,128)(2,1)S(1)}, bf16[2,16,4096]{2,1,0:T(8,128)(2,1)S(1)}, u32[]{:S(2)}, u32[]{:S(2)}) collective-permute-start(bf16[2,16,4096]{2,1,0:T(8,128)(2,1)S(1)} %get-tuple-element.49), channel_id=1, source_target_pairs={{0,48},{8,72},{16,0},{24,88},{32,16},{40,104},{48,32},{56,120},{64... | collective-permute-start | bytes 786440 | tf_op jit(solution)/shard_map/ppermute | solution.py:35
  71.9 3.2 %collective-permute-start.22 = (bf16[2,16,4096]{2,1,0:T(8,128)(2,1)S(1)}, bf16[2,16,4096]{2,1,0:T(8,128)(2,1)S(1)}, u32[]{:S(2)}, u32[]{:S(2)}) collective-permute-start(bf16[2,16,4096]{2,1,0:T(8,128)(2,1)S(1)} %get-tuple-element.46.refs_5_), channel_id=1, source_target_pairs={{0,32},{16,48},{32,0},{48,16},{64,96},{80,112},{96,64},{112,80},{1... | collective-permute-start | bytes 786440 | tf_op jit(solution)/shard_map/ppermute | solution.py:35
  75.2 0.2 chip_sum.2
  75.4 0.4 collective-permute-start.16
  75.8 2.9 %collective-permute-start.17 = (bf16[2,16,4096]{2,1,0:T(8,128)(2,1)S(1)}, bf16[2,16,4096]{2,1,0:T(8,128)(2,1)S(1)}, u32[]{:S(2)}, u32[]{:S(2)}) collective-permute-start(bf16[2,16,4096]{2,1,0:T(8,128)(2,1)S(1)} %get-tuple-element.40), channel_id=1, source_target_pairs={{0,48},{8,72},{16,0},{24,88},{32,16},{40,104},{48,32},{56,120},{64... | collective-permute-start | bytes 786440 | tf_op jit(solution)/shard_map/ppermute | solution.py:35
  78.7 2.9 %collective-permute-start.18 = (bf16[2,16,4096]{2,1,0:T(8,128)(2,1)S(1)}, bf16[2,16,4096]{2,1,0:T(8,128)(2,1)S(1)}, u32[]{:S(2)}, u32[]{:S(2)}) collective-permute-start(bf16[2,16,4096]{2,1,0:T(8,128)(2,1)S(1)} %get-tuple-element.37.refs_0_), channel_id=1, source_target_pairs={{0,32},{16,48},{32,0},{48,16},{64,96},{80,112},{96,64},{112,80},{1... | collective-permute-start | bytes 786440 | tf_op jit(solution)/shard_map/ppermute | solution.py:35
  81.6 0.1 collective-permute-done.22.refs_9_
  81.8 2.7 %collective-permute-done.16.refs_2_ = bf16[2,16,4096]{2,1,0:T(8,128)(2,1)S(1)} collective-permute-done((bf16[2,16,4096]{2,1,0:T(8,128)(2,1)S(1)}, bf16[2,16,4096]{2,1,0:T(8,128)(2,1)S(1)}, u32[]{:S(2)}, u32[]{:S(2)}) %collective-permute-start.16) | collective-permute-done | bytes 262176 | tf_op jit(solution)/shard_map/ppermute | solution.py:35
  84.5 0.0 collective-permute-done.17.refs_3_
  84.5 4.0 %collective-permute-done.18.refs_4_ = bf16[2,16,4096]{2,1,0:T(8,128)(2,1)S(1)} collective-permute-done((bf16[2,16,4096]{2,1,0:T(8,128)(2,1)S(1)}, bf16[2,16,4096]{2,1,0:T(8,128)(2,1)S(1)}, u32[]{:S(2)}, u32[]{:S(2)}) %collective-permute-start.18) | collective-permute-done | bytes 262176 | tf_op jit(solution)/shard_map/ppermute | solution.py:35
  88.5 0.3 stage_sum.1
  88.8 2.5 %collective-permute-start.23 = (bf16[16,8192]{1,0:T(8,128)(2,1)S(1)}, bf16[16,8192]{1,0:T(8,128)(2,1)S(1)}, u32[]{:S(2)}, u32[]{:S(2)}) collective-permute-start(bf16[16,8192]{1,0:T(8,128)(2,1)S(1)} %get-tuple-element.51), channel_id=1, source_target_pairs={{0,64},{8,24},{16,80},{24,40},{32,96},{40,56},{48,112},{56,8},{64,... | collective-permute-start | bytes 786440 | tf_op jit(solution)/shard_map/ppermute | solution.py:35
  91.3 0.7 collective-permute-start.24
  91.9 0.7 collective-permute-start.25
  92.6 4.1 %collective-permute-done.23.q4 = bf16[16,8192]{1,0:T(8,128)(2,1)S(1)} collective-permute-done((bf16[16,8192]{1,0:T(8,128)(2,1)S(1)}, bf16[16,8192]{1,0:T(8,128)(2,1)S(1)}, u32[]{:S(2)}, u32[]{:S(2)}) %collective-permute-start.23) | collective-permute-done | bytes 262176 | tf_op jit(solution)/shard_map/ppermute | solution.py:35
  96.7 0.0 collective-permute-done.24.q5
  96.7 0.0 collective-permute-done.25.q6
  96.8 0.8 last_sum.1
  (18 shorter events, 0.1 us)
Async XLA Ops:
  0.6 12.8 %collective-permute-start.1 = (bf16[16,8192]{1,0:T(8,128)(2,1)}, bf16[16,8192]{1,0:T(8,128)(2,1)S(1)}, u32[]{:S(2)}, u32[]{:S(2)}) collective-permute-start(bf16[16,8192]{1,0:T(8,128)(2,1)} %bitcast.13), channel_id=1, source_target_pairs={{0,16},{8,40},{16,32},{24,56},{32,48},{40,8},{48,0},{56,24},{64,80... | collective-permute-start | bytes 786440 | tf_op jit(solution)/shard_map/ppermute | solution.py:35
  2.4 11.1 %collective-permute-start = (bf16[16,8192]{1,0:T(8,128)(2,1)}, bf16[16,8192]{1,0:T(8,128)(2,1)S(1)}, u32[]{:S(2)}, u32[]{:S(2)}) collective-permute-start(bf16[16,8192]{1,0:T(8,128)(2,1)} %bitcast.14), channel_id=1, source_target_pairs={{0,64},{8,24},{16,80},{24,40},{32,96},{40,56},{48,112},{56,8},{64,... | collective-permute-start | bytes 786440 | tf_op jit(solution)/shard_map/ppermute | solution.py:35
  5.4 15.8 %collective-permute-start.7 = (bf16[16,8192]{1,0:T(8,128)(2,1)}, bf16[16,8192]{1,0:T(8,128)(2,1)S(1)}, u32[]{:S(2)}, u32[]{:S(2)}) collective-permute-start(bf16[16,8192]{1,0:T(8,128)(2,1)} %bitcast.15), channel_id=1, source_target_pairs={{0,8},{8,0},{1,9},{9,1},{2,10},{10,2},{3,11},{11,3},{4,12},{12,4},... | collective-permute-start | bytes 786440 | tf_op jit(solution)/shard_map/ppermute | solution.py:39
  5.4 10.7 %collective-permute-start.3 = (bf16[16,8192]{1,0:T(8,128)(2,1)}, bf16[16,8192]{1,0:T(8,128)(2,1)S(1)}, u32[]{:S(2)}, u32[]{:S(2)}) collective-permute-start(bf16[16,8192]{1,0:T(8,128)(2,1)} %bitcast.16), channel_id=1, source_target_pairs={{0,32},{8,72},{16,48},{24,88},{32,0},{40,104},{48,16},{56,120},{64... | collective-permute-start | bytes 786440 | tf_op jit(solution)/shard_map/ppermute | solution.py:35
  8.3 9.8 %collective-permute-start.2 = (bf16[16,8192]{1,0:T(8,128)(2,1)}, bf16[16,8192]{1,0:T(8,128)(2,1)S(1)}, u32[]{:S(2)}, u32[]{:S(2)}) collective-permute-start(bf16[16,8192]{1,0:T(8,128)(2,1)} %bitcast.17), channel_id=1, source_target_pairs={{0,48},{8,56},{16,0},{24,8},{32,16},{40,24},{48,32},{56,40},{64,11... | collective-permute-start | bytes 786440 | tf_op jit(solution)/shard_map/ppermute | solution.py:35
  13.5 15.5 %copy-start.1 = (bf16[2,512,128]{2,1,0:T(8,128)(2,1)S(1)}, bf16[2,512,128]{2,1,0:T(8,128)(2,1)}, u32[]{:S(2)}) copy-start(bf16[2,512,128]{2,1,0:T(8,128)(2,1)} %observed_ref.1) | copy-start | bytes 786436
  13.5 15.5 %copy-start.2 = (s32[512,64]{0,1:T(8,128)S(1)}, s32[512,64]{0,1:T(8,128)}, u32[]{:S(2)}) copy-start(s32[512,64]{0,1:T(8,128)} %param.6) | copy-start | bytes 393220
  13.5 18.1 %slice-start = ((s8[16777216]{0:T(1024)(128)(4,1)}), s8[4194304]{0:T(1024)(128)(4,1)S(1)}, s32[]{:S(2)}) async-start(s8[16777216]{0:T(1024)(128)(4,1)} %bitcast.11), calls=%async_computation.2 | async-start | bytes 8388608
  13.5 18.1 %slice-start.1 = ((s8[16777216]{0:T(1024)(128)(4,1)}), s8[4194304]{0:T(1024)(128)(4,1)S(1)}, s32[]{:S(2)}) async-start(s8[16777216]{0:T(1024)(128)(4,1)} %bitcast.11), calls=%async_computation.3 | async-start | bytes 8388608
  13.5 18.1 %slice-start.2 = ((s8[16777216]{0:T(1024)(128)(4,1)}), s8[4194304]{0:T(1024)(128)(4,1)S(1)}, s32[]{:S(2)}) async-start(s8[16777216]{0:T(1024)(128)(4,1)} %bitcast.11), calls=%async_computation.4 | async-start | bytes 8388608
  13.6 18.1 %copy-start = (bf16[2,8192,8]{1,2,0:T(8,128)(2,1)S(1)}, bf16[2,8192,8]{1,2,0:T(8,128)(2,1)}, u32[]{:S(2)}) copy-start(bf16[2,8192,8]{1,2,0:T(8,128)(2,1)} %param.7) | copy-start | bytes 786436
  13.6 9.2 %collective-permute-start.5 = (bf16[16,8192]{1,0:T(8,128)(2,1)S(1)}, bf16[16,8192]{1,0:T(8,128)(2,1)S(1)}, u32[]{:S(2)}, u32[]{:S(2)}) collective-permute-start(bf16[16,8192]{1,0:T(8,128)(2,1)S(1)} %pick.2), channel_id=1, source_target_pairs={{0,48},{8,72},{16,0},{24,88},{32,16},{40,104},{48,32},{56,120},{64... | collective-permute-start | bytes 786440 | tf_op jit(solution)/shard_map/ppermute | solution.py:35
  16.1 6.1 %collective-permute-start.11 = (bf16[16,8192]{1,0:T(8,128)(2,1)S(1)}, bf16[16,8192]{1,0:T(8,128)(2,1)S(1)}, u32[]{:S(2)}, u32[]{:S(2)}) collective-permute-start(bf16[16,8192]{1,0:T(8,128)(2,1)S(1)} %collective-permute-done.3.refs_4_), channel_id=1, source_target_pairs={{0,8},{8,0},{1,9},{9,1},{2,10},{10,2},{3,11},{11,3},{4,12},{12,4},... | collective-permute-start | bytes 786440 | tf_op jit(solution)/shard_map/ppermute | solution.py:39
  18.1 4.1 %collective-permute-start.10 = (bf16[16,8192]{1,0:T(8,128)(2,1)S(1)}, bf16[16,8192]{1,0:T(8,128)(2,1)S(1)}, u32[]{:S(2)}, u32[]{:S(2)}) collective-permute-start(bf16[16,8192]{1,0:T(8,128)(2,1)S(1)} %collective-permute-done.2.second.refs_3_), channel_id=1, source_target_pairs={{0,8},{8,0},{1,9},{9,1},{2,10},{10,2},{3,11},{11,3},{4,12},{12,4},... | collective-permute-start | bytes 786440 | tf_op jit(solution)/shard_map/ppermute | solution.py:39
  18.2 8.0 %collective-permute-start.6 = (bf16[16,8192]{1,0:T(8,128)(2,1)S(1)}, bf16[16,8192]{1,0:T(8,128)(2,1)S(1)}, u32[]{:S(2)}, u32[]{:S(2)}) collective-permute-start(bf16[16,8192]{1,0:T(8,128)(2,1)S(1)} %pick.3), channel_id=1, source_target_pairs={{0,32},{8,72},{16,48},{24,88},{32,0},{40,104},{48,16},{56,120},{64... | collective-permute-start | bytes 786440 | tf_op jit(solution)/shard_map/ppermute | solution.py:35
  21.3 7.7 %collective-permute-start.4 = (bf16[16,8192]{1,0:T(8,128)(2,1)S(1)}, bf16[16,8192]{1,0:T(8,128)(2,1)S(1)}, u32[]{:S(2)}, u32[]{:S(2)}) collective-permute-start(bf16[16,8192]{1,0:T(8,128)(2,1)S(1)} %collective-permute-done.first.refs_1_), channel_id=1, source_target_pairs={{0,16},{8,72},{16,32},{24,88},{32,48},{40,104},{48,0},{56,120},{64... | collective-permute-start | bytes 786440 | tf_op jit(solution)/shard_map/ppermute | solution.py:35
  22.2 9.3 %collective-permute-start.9 = (bf16[16,8192]{1,0:T(8,128)(2,1)S(1)}, bf16[16,8192]{1,0:T(8,128)(2,1)S(1)}, u32[]{:S(2)}, u32[]{:S(2)}) collective-permute-start(bf16[16,8192]{1,0:T(8,128)(2,1)S(1)} %collective-permute-done.1.second.refs_2_), channel_id=1, source_target_pairs={{0,8},{8,0},{1,9},{9,1},{2,10},{10,2},{3,11},{11,3},{4,12},{12,4},... | collective-permute-start | bytes 786440 | tf_op jit(solution)/shard_map/ppermute | solution.py:39
  22.2 9.3 %collective-permute-start.8 = (bf16[16,8192]{1,0:T(8,128)(2,1)S(1)}, bf16[16,8192]{1,0:T(8,128)(2,1)S(1)}, u32[]{:S(2)}, u32[]{:S(2)}) collective-permute-start(bf16[16,8192]{1,0:T(8,128)(2,1)S(1)} %collective-permute-done.first.refs_1_), channel_id=1, source_target_pairs={{0,8},{8,0},{1,9},{9,1},{2,10},{10,2},{3,11},{11,3},{4,12},{12,4},... | collective-permute-start | bytes 786440 | tf_op jit(solution)/shard_map/ppermute | solution.py:39
  22.7 8.8 %collective-permute-start.13 = (bf16[16,8192]{1,0:T(8,128)(2,1)S(1)}, bf16[16,8192]{1,0:T(8,128)(2,1)S(1)}, u32[]{:S(2)}, u32[]{:S(2)}) collective-permute-start(bf16[16,8192]{1,0:T(8,128)(2,1)S(1)} %collective-permute-done.5.refs_6_), channel_id=1, source_target_pairs={{0,8},{8,0},{1,9},{9,1},{2,10},{10,2},{3,11},{11,3},{4,12},{12,4},... | collective-permute-start | bytes 786440 | tf_op jit(solution)/shard_map/ppermute | solution.py:39
  26.2 5.4 %collective-permute-start.14 = (bf16[16,8192]{1,0:T(8,128)(2,1)S(1)}, bf16[16,8192]{1,0:T(8,128)(2,1)S(1)}, u32[]{:S(2)}, u32[]{:S(2)}) collective-permute-start(bf16[16,8192]{1,0:T(8,128)(2,1)S(1)} %collective-permute-done.6.refs_7_), channel_id=1, source_target_pairs={{0,8},{8,0},{1,9},{9,1},{2,10},{10,2},{3,11},{11,3},{4,12},{12,4},... | collective-permute-start | bytes 786440 | tf_op jit(solution)/shard_map/ppermute | solution.py:39
  29.0 2.6 %collective-permute-start.12 = (bf16[16,8192]{1,0:T(8,128)(2,1)S(1)}, bf16[16,8192]{1,0:T(8,128)(2,1)S(1)}, u32[]{:S(2)}, u32[]{:S(2)}) collective-permute-start(bf16[16,8192]{1,0:T(8,128)(2,1)S(1)} %collective-permute-done.4.refs_5_), channel_id=1, source_target_pairs={{0,8},{8,0},{1,9},{9,1},{2,10},{10,2},{3,11},{11,3},{4,12},{12,4},... | collective-permute-start | bytes 786440 | tf_op jit(solution)/shard_map/ppermute | solution.py:39
  29.0 2.7 %slice-start.3 = ((s8[16777216]{0:T(1024)(128)(4,1)}), s8[4194304]{0:T(1024)(128)(4,1)S(1)}, s32[]{:S(2)}) async-start(s8[16777216]{0:T(1024)(128)(4,1)} %bitcast.11), calls=%async_computation.5 | async-start | bytes 8388608
  31.5 20.7 %copy-start.3 = (s32[512]{0:T(512)S(1)}, s32[512]{0:T(512)}, u32[]{:S(2)}) copy-start(s32[512]{0:T(512)} %param.9) | copy-start | bytes 6148
  65.1 3.3 %collective-permute-start.19 = (bf16[8,16,4096]{2,1,0:T(8,128)(2,1)S(1)}, bf16[8,16,4096]{2,1,0:T(8,128)(2,1)S(1)}, u32[]{:S(2)}, u32[]{:S(2)}) collective-permute-start(bf16[8,16,4096]{2,1,0:T(8,128)(2,1)S(1)} %get-tuple-element.45), channel_id=1, source_target_pairs={{0,8},{8,0},{1,9},{9,1},{2,10},{10,2},{3,11},{11,3},{4,12},{12,4},... | collective-permute-start | bytes 3145736 | tf_op jit(solution)/shard_map/ppermute | solution.py:39
  67.8 7.4 %collective-permute-start.15 = (bf16[8,16,4096]{2,1,0:T(8,128)(2,1)S(1)}, bf16[8,16,4096]{2,1,0:T(8,128)(2,1)S(1)}, u32[]{:S(2)}, u32[]{:S(2)}) collective-permute-start(bf16[8,16,4096]{2,1,0:T(8,128)(2,1)S(1)} %get-tuple-element.36), channel_id=1, source_target_pairs={{0,8},{8,0},{1,9},{9,1},{2,10},{10,2},{3,11},{11,3},{4,12},{12,4},... | collective-permute-start | bytes 3145736 | tf_op jit(solution)/shard_map/ppermute | solution.py:39
  68.6 10.1 %collective-permute-start.20 = (bf16[2,16,4096]{2,1,0:T(8,128)(2,1)S(1)}, bf16[2,16,4096]{2,1,0:T(8,128)(2,1)S(1)}, u32[]{:S(2)}, u32[]{:S(2)}) collective-permute-start(bf16[2,16,4096]{2,1,0:T(8,128)(2,1)S(1)} %get-tuple-element.48), channel_id=1, source_target_pairs={{0,16},{8,72},{16,32},{24,88},{32,48},{40,104},{48,0},{56,120},{64... | collective-permute-start | bytes 786440 | tf_op jit(solution)/shard_map/ppermute | solution.py:35
  70.1 11.5 %collective-permute-start.21 = (bf16[2,16,4096]{2,1,0:T(8,128)(2,1)S(1)}, bf16[2,16,4096]{2,1,0:T(8,128)(2,1)S(1)}, u32[]{:S(2)}, u32[]{:S(2)}) collective-permute-start(bf16[2,16,4096]{2,1,0:T(8,128)(2,1)S(1)} %get-tuple-element.49), channel_id=1, source_target_pairs={{0,48},{8,72},{16,0},{24,88},{32,16},{40,104},{48,32},{56,120},{64... | collective-permute-start | bytes 786440 | tf_op jit(solution)/shard_map/ppermute | solution.py:35
  71.9 9.9 %collective-permute-start.22 = (bf16[2,16,4096]{2,1,0:T(8,128)(2,1)S(1)}, bf16[2,16,4096]{2,1,0:T(8,128)(2,1)S(1)}, u32[]{:S(2)}, u32[]{:S(2)}) collective-permute-start(bf16[2,16,4096]{2,1,0:T(8,128)(2,1)S(1)} %get-tuple-element.46.refs_5_), channel_id=1, source_target_pairs={{0,32},{16,48},{32,0},{48,16},{64,96},{80,112},{96,64},{112,80},{1... | collective-permute-start | bytes 786440 | tf_op jit(solution)/shard_map/ppermute | solution.py:35
  75.4 9.1 %collective-permute-start.16 = (bf16[2,16,4096]{2,1,0:T(8,128)(2,1)S(1)}, bf16[2,16,4096]{2,1,0:T(8,128)(2,1)S(1)}, u32[]{:S(2)}, u32[]{:S(2)}) collective-permute-start(bf16[2,16,4096]{2,1,0:T(8,128)(2,1)S(1)} %get-tuple-element.39), channel_id=1, source_target_pairs={{0,16},{8,72},{16,32},{24,88},{32,48},{40,104},{48,0},{56,120},{64... | collective-permute-start | bytes 786440 | tf_op jit(solution)/shard_map/ppermute | solution.py:35
  75.8 8.7 %collective-permute-start.17 = (bf16[2,16,4096]{2,1,0:T(8,128)(2,1)S(1)}, bf16[2,16,4096]{2,1,0:T(8,128)(2,1)S(1)}, u32[]{:S(2)}, u32[]{:S(2)}) collective-permute-start(bf16[2,16,4096]{2,1,0:T(8,128)(2,1)S(1)} %get-tuple-element.40), channel_id=1, source_target_pairs={{0,48},{8,72},{16,0},{24,88},{32,16},{40,104},{48,32},{56,120},{64... | collective-permute-start | bytes 786440 | tf_op jit(solution)/shard_map/ppermute | solution.py:35
  78.7 9.8 %collective-permute-start.18 = (bf16[2,16,4096]{2,1,0:T(8,128)(2,1)S(1)}, bf16[2,16,4096]{2,1,0:T(8,128)(2,1)S(1)}, u32[]{:S(2)}, u32[]{:S(2)}) collective-permute-start(bf16[2,16,4096]{2,1,0:T(8,128)(2,1)S(1)} %get-tuple-element.37.refs_0_), channel_id=1, source_target_pairs={{0,32},{16,48},{32,0},{48,16},{64,96},{80,112},{96,64},{112,80},{1... | collective-permute-start | bytes 786440 | tf_op jit(solution)/shard_map/ppermute | solution.py:35
  88.8 7.9 %collective-permute-start.23 = (bf16[16,8192]{1,0:T(8,128)(2,1)S(1)}, bf16[16,8192]{1,0:T(8,128)(2,1)S(1)}, u32[]{:S(2)}, u32[]{:S(2)}) collective-permute-start(bf16[16,8192]{1,0:T(8,128)(2,1)S(1)} %get-tuple-element.51), channel_id=1, source_target_pairs={{0,64},{8,24},{16,80},{24,40},{32,96},{40,56},{48,112},{56,8},{64,... | collective-permute-start | bytes 786440 | tf_op jit(solution)/shard_map/ppermute | solution.py:35
  91.3 5.5 %collective-permute-start.24 = (bf16[16,8192]{1,0:T(8,128)(2,1)S(1)}, bf16[16,8192]{1,0:T(8,128)(2,1)S(1)}, u32[]{:S(2)}, u32[]{:S(2)}) collective-permute-start(bf16[16,8192]{1,0:T(8,128)(2,1)S(1)} %get-tuple-element.52), channel_id=1, source_target_pairs={{8,56},{24,8},{40,24},{56,40},{72,120},{88,72},{104,88},{120,104},... | collective-permute-start | bytes 786440 | tf_op jit(solution)/shard_map/ppermute | solution.py:35
  91.9 4.8 %collective-permute-start.25 = (bf16[16,8192]{1,0:T(8,128)(2,1)S(1)}, bf16[16,8192]{1,0:T(8,128)(2,1)S(1)}, u32[]{:S(2)}, u32[]{:S(2)}) collective-permute-start(bf16[16,8192]{1,0:T(8,128)(2,1)S(1)} %get-tuple-element.53), channel_id=1, source_target_pairs={{8,40},{24,56},{40,8},{56,24},{72,104},{88,120},{104,72},{120,88},... | collective-permute-start | bytes 786440 | tf_op jit(solution)/shard_map/ppermute | solution.py:35
